TPU v7x, 128 devices: a whole 4x4x4 slice. The times are simulated.
128 devices in a mesh: ctx: 32 (over y, z, core), exp: 4 (over x).
Axes of the slice: x: 4, y: 4, z: 4, core: 2. Of those that a mesh axis runs over, the one named last changes fastest.
Arguments:
- inputs: bfloat16 [4096, 4096], P('ctx', 'exp'), may hold values from -6 to 6
- gate_input: bfloat16 [4096, 4096], P('ctx', 'exp')
- b_proj: bfloat16 [4096, 128], P('ctx'), may hold values from -0.5 to 0.5
- c_proj: bfloat16 [4096, 128], P('ctx'), may hold values from -6 to 6
- step_size: float32 [64, 4096], P('exp', 'ctx'), may hold values from 0.03 to 0.3
- decay_rate: float32 [64, 4096], P('exp', 'ctx'), as said below
- skip_gain: float32 [64], P('exp'), may hold values from 0.5 to 2
- start_state: float32 [64, 64, 128], P('exp'), may hold values from -3 to 3
- norm_gain: float32 [4096], P('exp'), may hold values from 0.5 to 1.5
- out_proj: bfloat16 [4096, 4096], P('exp', 'ctx'), may hold values from -0.09375 to 0.09375
- residual: bfloat16 [4096, 4096], P('ctx'), may hold values from -6 to 6
- moe_gain: float32 [4096], replicated, may hold values from 0.5 to 1.5
- w_gate: bfloat16 [32, 4096, 3584], P('ctx', None, 'exp'), may hold values from -0.09375 to 0.09375
- w_up: bfloat16 [32, 4096, 3584], P('ctx', None, 'exp'), may hold values from -0.09375 to 0.09375
- w_down: bfloat16 [32, 3584, 4096], P('ctx', 'exp'), may hold values from -0.0625 to 0.0625
- route_ids: int32 [4096, 2], P('ctx'), may hold values from 0 to 15, all different within a row; in each aligned block of 32 rows (0 to 31, 32 to 63, ...) at most 8 rows name the same one
- route_gates: float32 [4096, 2], P('ctx'), may hold values from 0.3 to 1
Outputs:
- output: bfloat16 [4096, 4096], P(('ctx', 'exp'))
Inputs may be any that keep to these rules, and one draw needn't show every extreme that they name: `route_ids`: each row names two different experts. In each aligned block of 32 rows no expert is named more than 8 times, a bound that some block reaches. `decay_rate`: Non-negative.
All inputs are finite; a program needn't handle non-finite values.
Results may differ from a plain program's by a relative error of at most 0.02.
Values may be sent and summed in bfloat16 or wider, within the bound.
A program may use at most 128 MiB of HBM per device.

v0:
```python
import jax
import jax.numpy as jnp
from jax import lax
from jax.sharding import PartitionSpec as P

PAIR = 2
eps_norm = 1e-05
top_precision = lax.Precision.HIGHEST


def entering(x, axis, join, neutral):
    place = lax.axis_index(axis)
    decay, state = x
    packed = jnp.concatenate(
        [state, jnp.broadcast_to(decay[:, None, None], (state.shape[0], 1, state.shape[2]))], axis=1
    )
    gathered = lax.all_gather(packed.astype(jnp.bfloat16), axis)
    start = jax.tree.map(lambda a, e: jnp.zeros_like(a) + jnp.asarray(e, a.dtype), x, neutral)

    def one(hop, carry):
        block = lax.dynamic_index_in_dim(gathered, hop, 0, False).astype(jnp.float32)
        return join(carry, (block[:, -1, 0], block[:, :-1, :]))

    return lax.fori_loop(0, place, one, start)


def later_state(earlier, later):
    first_decay, first_state = earlier
    second_decay, second_state = later
    return (first_decay * second_decay, second_decay[:, None, None] * first_state + second_state)


def route_ranks(quarter_ids, experts):
    flattened = quarter_ids.reshape(-1)
    onehot = (flattened[:, None] == jnp.arange(experts, dtype=jnp.int32)[None, :]).astype(jnp.int32)
    running = jnp.cumsum(onehot, axis=0)
    rank_ids = jnp.sum(onehot * running, axis=1) - 1
    return (flattened, rank_ids)


def place_rows(normed, quarter_ids, experts, capacity):
    flattened, rank_ids = route_ranks(quarter_ids, experts)
    slot_ids = rank_ids * experts + flattened
    matches = (
        jnp.arange(capacity * experts, dtype=jnp.int32)[:, None] == slot_ids[None, :]
    ).astype(jnp.bfloat16)
    doubled = jnp.repeat(normed, quarter_ids.shape[1], axis=0)
    placed = jnp.dot(matches, doubled, preferred_element_type=jnp.float32).astype(jnp.bfloat16)
    return placed.reshape(capacity, experts, normed.shape[1])


def rms_rows(values, gain_vec):
    scaling = lax.rsqrt(jnp.mean(values * values, axis=1, keepdims=True) + eps_norm)
    return (values * scaling * gain_vec[None, :]).astype(jnp.bfloat16)


def local(
    inputs,
    gate_input,
    b_proj,
    c_proj,
    step_size,
    decay_rate,
    skip_gain,
    start_state,
    norm_gain,
    out_proj,
    residual,
    moe_gain,
    w_gate,
    w_up,
    w_down,
    route_ids,
    route_gates,
):
    tok_ctx = inputs.shape[0]
    head_count = step_size.shape[0]
    head_dim = inputs.shape[1] // head_count
    model_width = residual.shape[1]
    n_ctx = lax.axis_size("ctx")
    n_exp = lax.axis_size("exp")
    experts = n_ctx // PAIR
    tok_quarter = tok_ctx // n_exp
    capacity = 4 * tok_quarter // experts
    x_local = inputs.astype(jnp.float32).reshape(tok_ctx, head_count, head_dim)
    b_local = b_proj.astype(jnp.float32)
    c_local = c_proj.astype(jnp.float32)
    cumulative = jnp.cumsum(decay_rate, axis=1)
    span_total = cumulative[:, -1]
    sequence_indices = jnp.arange(tok_ctx, dtype=jnp.int32)
    causal = sequence_indices[:, None] >= sequence_indices[None, :]
    spread = jnp.where(causal[None], cumulative[:, :, None] - cumulative[:, None, :], 0.0)
    scores = jnp.dot(c_local, b_local.T, precision=top_precision)
    mixing = jnp.where(causal[None], jnp.exp(-spread), 0.0) * scores[None] * step_size[:, None, :]
    inside_part = jnp.einsum("hts,shp->thp", mixing, x_local, precision=top_precision)
    ending = jnp.exp(-(span_total[:, None] - cumulative)) * step_size
    local_state = jnp.einsum("hs,shp,sn->hpn", ending, x_local, b_local, precision=top_precision)
    prior_decay, prior_state = entering(
        (jnp.exp(-span_total), local_state),
        "ctx",
        later_state,
        (jnp.ones_like(span_total), jnp.zeros_like(local_state)),
    )
    incoming = prior_state + prior_decay[:, None, None] * start_state
    carried = (
        jnp.einsum("hpn,tn->thp", incoming, c_local, precision=top_precision)
        * jnp.exp(-cumulative).T[:, :, None]
    )
    ssm_out = inside_part + carried + skip_gain[None, :, None] * x_local
    gated_out = ssm_out.reshape(tok_ctx, head_count * head_dim) * jax.nn.silu(
        gate_input.astype(jnp.float32)
    )
    squares = lax.psum(jnp.sum(gated_out * gated_out, axis=1), "exp")
    scaling = lax.rsqrt(squares / (head_count * head_dim * n_exp) + eps_norm)
    normed_mix = (gated_out * scaling[:, None] * norm_gain[None, :]).astype(jnp.bfloat16)
    partial_value = jnp.dot(
        normed_mix,
        lax.all_gather(out_proj, "ctx", axis=1, tiled=True),
        preferred_element_type=jnp.float32,
    )
    gate_rows = w_gate[0]
    up_rows = w_up[0]
    down_rows = w_down[0]
    piece_width = gate_rows.shape[1]
    first_row = lax.axis_index("exp") * tok_quarter
    own_ids = lax.dynamic_slice_in_dim(route_ids, first_row, tok_quarter, 0)
    own_gates = lax.dynamic_slice_in_dim(route_gates, first_row, tok_quarter, 0)
    mixed_all = lax.psum(partial_value.astype(jnp.bfloat16), "exp").astype(jnp.float32)
    hidden_all = residual.astype(jnp.float32) + mixed_all
    moe_all = rms_rows(hidden_all, moe_gain)

    def place_quarter(quarter_rows, quarter_ids):
        return place_rows(quarter_rows, quarter_ids, experts, capacity)

    placed = jax.vmap(place_quarter)(
        moe_all.reshape(n_exp, tok_quarter, model_width),
        route_ids.reshape(n_exp, tok_quarter, route_ids.shape[1]),
    )
    placed = placed.reshape(n_exp * capacity, experts, model_width)
    outgoing = jnp.repeat(placed, PAIR, axis=1)
    arrived = lax.all_to_all(outgoing, "ctx", split_axis=1, concat_axis=1, tiled=True)
    flattened = arrived.reshape(-1, model_width)
    gate_val = jnp.dot(flattened, gate_rows, preferred_element_type=jnp.float32)
    up_val = jnp.dot(flattened, up_rows, preferred_element_type=jnp.float32)
    activated = (jax.nn.silu(gate_val) * up_val).astype(jnp.bfloat16)
    hidden = activated.reshape(arrived.shape[0], arrived.shape[1], piece_width)
    hidden_own = lax.dynamic_slice_in_dim(hidden_all, first_row, tok_quarter, 0)
    product = jnp.dot(
        hidden.reshape(-1, piece_width), down_rows, preferred_element_type=jnp.float32
    )
    rounded = lax.optimization_barrier(product.astype(jnp.bfloat16)).astype(jnp.float32)
    summed = lax.psum_scatter(
        rounded.reshape(lax.axis_size("exp") * capacity, hidden.shape[1], model_width).astype(
            jnp.bfloat16
        ),
        "exp",
        scatter_dimension=0,
        tiled=True,
    )
    halves = lax.all_to_all(summed, "ctx", split_axis=1, concat_axis=1, tiled=True)
    flattened, rank_ids = route_ranks(own_ids, experts)
    base_rows = rank_ids * n_ctx + flattened * PAIR
    fetch_rows = base_rows[:, None] + jnp.arange(PAIR, dtype=jnp.int32)[None, :]
    fetched = halves.reshape(capacity * n_ctx, model_width)[fetch_rows]
    expert_out = jnp.sum(fetched.astype(jnp.float32), axis=1)
    weighted = expert_out * own_gates.reshape(-1)[:, None]
    moe_out = jnp.sum(weighted.reshape(tok_quarter, -1, model_width), axis=1)
    return (hidden_own + moe_out).astype(jnp.bfloat16)


def solution(mesh):
    in_specs = (
        P("ctx", "exp"),
        P("ctx", "exp"),
        P("ctx", None),
        P("ctx", None),
        P("exp", "ctx"),
        P("exp", "ctx"),
        P("exp"),
        P("exp", None, None),
        P("exp"),
        P("exp", "ctx"),
        P("ctx", None),
        P(),
        P("ctx", None, "exp"),
        P("ctx", None, "exp"),
        P("ctx", "exp", None),
        P("ctx", None),
        P("ctx", None),
    )
    out_specs = P(("ctx", "exp"), None)
    return jax.shard_map(local, mesh=mesh, in_specs=in_specs, out_specs=out_specs, check_vma=False)
```

profile of v0, /device:TPU:1, one launch (start us, length us, event | category | flops | bytes accessed | tf_op | source)
XLA Modules:
  0.0 688.3 jit_solution(15999288479080339872)
XLA Ops:
  12.6 55.4 %all-gather.3.cloned.1.call-done = bf16[32,16,65,128]{3,1,2,0:T(8,128)(2,1)} async-done(((bf16[1,16,65,128]{3,1,2,0:T(8,128)(2,1)}), bf16[32,16,65,128]{3,1,2,0:T(8,128)(2,1)}) %all-gather.3.cloned.1.call-update) | async-done | bytes 8519696 | tf_op jit(solution)/shard_map/all_gather | solution.py:17
  68.1 2.4 broadcast_in_dim.28
  70.5 7.9 %while.12 = (s32[]{:T(128)}, f32[16]{0:T(128)S(1)}, f32[16,64,128]{0,2,1:T(8,128)}, s32[]{:T(128)}, bf16[32,16,65,128]{3,1,2,0:T(8,128)(2,1)}, /*index=5*/s32[]{:T(128)}, s32[]{:T(128)}, s32[]{:T(128)}) while((s32[]{:T(128)}, f32[16]{0:T(128)S(1)}, f32[16,64,128]{0,2,1:T(8,128)}, s32[]{:T(128)}, bf16[32,16,65,128]{3,1,2,0:T(8,128)(2,1)}, ...), condition=%wide.region_2.3_spmd, body=%wide.region_1.2_spmd.sunk | while | flops 395285 | bytes 3437051 | solution.py:24
  71.5 1.4 copy.132
  73.4 5.0 slice_add_fusion.2
  78.5 3.1 copy.112
  82.1 1.4 fusion.9
  83.9 8.4 %psum.14 = f32[128]{0:T(128)S(1)} all-reduce(f32[128]{0:T(128)S(1)} %multiply_reduce_fusion.2), channel_id=1, replica_groups=mesh['ctx'=32,'exp'=4] {'exp'}, use_global_device_ids=true, to_apply=%region_4.5 | all-reduce | flops 128 | bytes 1024 | tf_op jit(solution)/shard_map/psum | solution.py:113
  92.3 37.1 %all-gather.5.cloned.1.call-done = bf16[1024,4096]{1,0:T(8,128)(2,1)} async-done(((bf16[1024,128]{1,0:T(8,128)(2,1)}), bf16[1024,4096]{1,0:T(8,128)(2,1)}) %all-gather.5.cloned.1.call-update) | async-done | bytes 8388624 | tf_op jit(solution)/shard_map/all_gather | solution.py:118
  129.5 5.8 convolution_convert_fusion.2
  136.3 240.4 %all-reduce.2.cloned.1.call-done = bf16[128,4096]{1,0:T(8,128)(2,1)} async-done(((bf16[128,4096]{1,0:T(8,128)(2,1)}), bf16[128,4096]{1,0:T(8,128)(2,1)}) %all-reduce.2.cloned.1.call-update) | async-done | bytes 1048592 | tf_op jit(solution)/shard_map/psum | solution.py:128
  376.8 3.0 convert_add_fusion
  380.2 3.4 broadcast_in_dim.30
  383.6 2.7 reshape.163
  386.4 1.4 convolution_convert_fusion.1
  387.8 2.3 copy.117
  390.1 4.3 broadcast_in_dim.31
  394.3 105.3 %all_to_all.10 = bf16[32,32,4096]{2,0,1:T(8,128)(2,1)} all-to-all(bf16[32,32,4096]{2,0,1:T(8,128)(2,1)} %bitcast.70), channel_id=1, replica_groups=mesh['ctx'=32,'exp'=4] {'ctx'}, dimensions={1} | all-to-all | bytes 16777216 | tf_op jit(solution)/shard_map/all_to_all | solution.py:141
  499.6 11.3 %copy.118 = bf16[32,32,4096]{2,1,0:T(8,128)(2,1)} copy(bf16[32,32,4096]{2,0,1:T(8,128)(2,1)} %all_to_all.10) | data formatting | bytes 16777216 | tf_op jit(solution)/shard_map/all_to_all | solution.py:141
  511.0 12.7 %fusion.2 = f32[1024,896]{1,0:T(8,128)S(1)} fusion(bf16[1024,4096]{1,0:T(8,128)(2,1)} %bitcast.72, bf16[1,4096,896]{2,1,0:T(8,128)(2,1)} %param.32), kind=kOutput, calls=%fused_computation.8 | convolution fusion | flops 7516192768 | bytes 19398656 | tf_op jit(solution)/shard_map/dot_general | solution.py:144
  523.7 9.2 %multiply_convert_fusion = bf16[1024,896]{1,0:T(8,128)(2,1)S(1)} fusion(f32[1024,896]{1,0:T(8,128)S(1)} %fusion.2, bf16[1024,4096]{1,0:T(8,128)(2,1)S(1)} %bitcast.73, bf16[1,4096,896]{2,1,0:T(8,128)(2,1)S(1)} %bitcast.81), kind=kOutput, calls=%fused_computation.14 | convolution fusion | flops 7521697792 | bytes 21233664 | tf_op jit(solution)/shard_map/dot_general | solution.py:143
  532.9 11.3 %convolution_convert_fusion = bf16[1024,4096]{1,0:T(8,128)(2,1)} fusion(bf16[1024,896]{1,0:T(8,128)(2,1)S(1)} %multiply_convert_fusion, bf16[1,896,4096]{2,1,0:T(8,128)(2,1)S(1)} %bitcast.83), kind=kOutput, calls=%fused_computation.6 | convolution fusion | flops 7520387072 | bytes 17563648 | tf_op jit(solution)/shard_map/dot_general | solution.py:148
  544.1 11.3 %copy.130 = bf16[4,8,32,4096]{3,1,2,0:T(8,128)(2,1)} copy(bf16[4,8,32,4096]{3,2,1,0:T(8,128)(2,1)} %bitcast.74) | data formatting | bytes 16777216
  555.5 77.8 %reduce-scatter.4.cloned.1.call-done = bf16[8,131072]{1,0:T(8,128)(2,1)} async-done(((bf16[32,131072]{1,0:T(8,128)(2,1)}), bf16[8,131072]{1,0:T(8,128)(2,1)}) %reduce-scatter.4.cloned.1.call-update) | async-done | bytes 2097168
  633.2 8.1 %all-to-all-start.1 = ((bf16[8,32,4096]{2,0,1:T(8,128)(2,1)}), bf16[8,32,4096]{2,0,1:T(8,128)(2,1)}, u32[]{:S(2)}, u32[]{:S(2)}) async-start(bf16[8,32,4096]{2,0,1:T(8,128)(2,1)} %bitcast.76), calls=%async_computation.1 | async-start | bytes 4194304 | tf_op jit(solution)/shard_map/all_to_all | solution.py:160
  642.4 27.1 %all-to-all-done.1 = bf16[8,32,4096]{2,0,1:T(8,128)(2,1)} async-done(((bf16[8,32,4096]{2,0,1:T(8,128)(2,1)}), bf16[8,32,4096]{2,0,1:T(8,128)(2,1)}, u32[]{:S(2)}, u32[]{:S(2)}) %all-to-all-start.1) | async-done | bytes 2097184 | tf_op jit(solution)/shard_map/all_to_all | solution.py:160
  669.5 2.7 copy.120
  672.3 1.2 gather_fusion
  673.5 1.3 reshape.178
  674.8 2.7 reduce_sum.60
  678.2 1.4 multiply_reduce_fusion.1
  679.6 1.8 add_convert_fusion
  (87 shorter events, 11.6 us)
Async XLA Ops:
  6.5 3.1 copy-start
  6.5 61.5 %all-gather.3.cloned.1.call-start = ((), (), s32[]{:S(2)}) async-start(), calls=%async_computation.3 | async-start | bytes 8785920 | tf_op jit(solution)/shard_map/all_gather | solution.py:17
  10.9 118.5 %all-gather.5.cloned.1.call-start = ((), (), s32[]{:S(2)}) async-start(), calls=%async_computation.4 | async-start | bytes 8650752 | tf_op jit(solution)/shard_map/all_gather | solution.py:118
  11.7 365.1 %all-reduce.2.cloned.1.call-start = ((), (), s32[]{:S(2)}) async-start(), calls=%async_computation.5 | async-start | bytes 2097152 | tf_op jit(solution)/shard_map/psum | solution.py:128
  78.4 3.1 copy-start.5
  78.4 3.1 copy-start.7
  78.4 3.6 copy-start.9
  78.4 3.6 copy-start.13
  78.5 5.2 copy-start.6
  81.5 47.9 %copy-start.12 = (f32[1024]{0:T(1024)S(1)}, f32[1024]{0:T(1024)}, u32[]{:S(2)}) copy-start(f32[1024]{0:T(1024)} %param.27) | copy-start | bytes 12292
  92.3 43.3 %copy-start.10 = (s32[128,2]{0,1:T(2,128)S(1)}, s32[128,2]{0,1:T(2,128)}, u32[]{:S(2)}) copy-start(s32[128,2]{0,1:T(2,128)} %param.34) | copy-start | bytes 3076
  92.3 284.4 %copy-start.3 = (bf16[128,4096]{1,0:T(8,128)(2,1)S(1)}, bf16[128,4096]{1,0:T(8,128)(2,1)}, u32[]{:S(2)}) copy-start(bf16[128,4096]{1,0:T(8,128)(2,1)} %param.29) | copy-start | bytes 3145732
  135.3 244.5 %copy-start.8 = (f32[4096]{0:T(1024)S(1)}, f32[4096]{0:T(1024)}, u32[]{:S(2)}) copy-start(f32[4096]{0:T(1024)} %param.30) | copy-start | bytes 49156
  135.3 498.0 %reduce-scatter.4.cloned.1.call-start = ((), (), s32[]{:S(2)}) async-start(), calls=%async_computation.6 | async-start | bytes 10485760
  376.8 3.0 copy-start.4
  499.6 24.0 %slice-start = ((s8[7340032]{0:T(1024)(128)(4,1)}), s8[3145728]{0:T(1024)(128)(4,1)S(1)}, s32[]{:S(2)}) async-start(s8[7340032]{0:T(1024)(128)(4,1)} %bitcast.80), calls=%async_computation.7 | async-start | bytes 6291456
  511.0 12.7 %copy-start.2 = (bf16[32,32,4096]{2,1,0:T(8,128)(2,1)S(1)}, bf16[32,32,4096]{2,1,0:T(8,128)(2,1)}, u32[]{:S(2)}) copy-start(bf16[32,32,4096]{2,1,0:T(8,128)(2,1)} %copy.118) | copy-start | bytes 25165828
  511.0 12.7 %slice-start.1 = ((s8[7340032]{0:T(1024)(128)(4,1)}), s8[4194304]{0:T(1024)(128)(4,1)S(1)}, s32[]{:S(2)}) async-start(s8[7340032]{0:T(1024)(128)(4,1)} %bitcast.80), calls=%async_computation.8 | async-start | bytes 8388608
  511.0 21.9 %slice-start.2 = ((s8[7340032]{0:T(1024)(128)(4,1)}), s8[4194304]{0:T(1024)(128)(4,1)S(1)}, s32[]{:S(2)}) async-start(s8[7340032]{0:T(1024)(128)(4,1)} %bitcast.82), calls=%async_computation.9 | async-start | bytes 8388608
  523.7 9.2 %slice-start.3 = ((s8[7340032]{0:T(1024)(128)(4,1)}), s8[3145728]{0:T(1024)(128)(4,1)S(1)}, s32[]{:S(2)}) async-start(s8[7340032]{0:T(1024)(128)(4,1)} %bitcast.82), calls=%async_computation.10 | async-start | bytes 6291456
  555.5 86.8 %copy-start.11 = (f32[128,2]{0,1:T(2,128)S(1)}, f32[128,2]{0,1:T(2,128)}, u32[]{:S(2)}) copy-start(f32[128,2]{0,1:T(2,128)} %param.35) | copy-start | bytes 3076
  633.2 36.3 %all-to-all-start.1 = ((bf16[8,32,4096]{2,0,1:T(8,128)(2,1)}), bf16[8,32,4096]{2,0,1:T(8,128)(2,1)}, u32[]{:S(2)}, u32[]{:S(2)}) async-start(bf16[8,32,4096]{2,0,1:T(8,128)(2,1)} %bitcast.76), calls=%async_computation.1 | async-start | bytes 4194304 | tf_op jit(solution)/shard_map/all_to_all | solution.py:160
  673.5 8.0 %copy-start.1 = (bf16[128,128]{1,0:T(8,128)(2,1)S(1)}, bf16[128,128]{1,0:T(8,128)(2,1)}, u32[]{:S(2)}) copy-start(bf16[128,128]{1,0:T(8,128)(2,1)} %param.21) | copy-start | bytes 98308
Sparse Core Ops, SparseCore 0:
  11.0 56.9 all-gather.2
  70.2 59.1 all-gather.4
  135.4 241.3 all-reduce.1
  555.6 77.6 reduce-scatter.3
where the time goes:
time: 696 us; the launch traced here: 688 us
  waiting for transfers between devices  439 us (63%)
  blocking collectives  114 us (16%)
  local copies, waits for them, and re-layouts  52.4 us (8%)
  matrix products  43.4 us (6%)
  other arithmetic  17.9 us (3%)
  between operations  13.8 us (2%)
  starting transfers between devices  8.55 us (1%)
    psum x1, waiting for transfers between devices, local(): lax.psum(partial_value.astype(jnp.bfloat16), 'exp').astype(jnp.float32)  240 us
    all_to_all x1, blocking collectives, local(): lax.all_to_all(outgoing, 'ctx', split_axis=1, concat_axis=1, tiled=True)  105 us
    unnamed x5, waiting for transfers between devices  78.5 us
    all_gather x1, waiting for transfers between devices, entering(): gathered = lax.all_gather(packed.astype(jnp.bfloat16), axis)  55.4 us
    all_gather x1, waiting for transfers between devices, local(): lax.all_gather(out_proj, 'ctx', axis=1, tiled=True)  37.1 us
    all_to_all x1, waiting for transfers between devices, local(): lax.all_to_all(summed, 'ctx', split_axis=1, concat_axis=1, tiled=True)  27.1 us
  transfers between devices with their start and end apart: 5, of which 5 were waited for; matrix products, arithmetic and copies ran while one was open for 3% of the time, Pallas kernels for 0%

commit v1 on v0

--- a/solution.py
+++ b/solution.py
@@ -6,6 +6,14 @@
 PAIR = 2
 eps_norm = 1e-05
 top_precision = lax.Precision.HIGHEST
+
+
+def tiled_gather(value, axis, dim):
+    length = lax.axis_size(axis)
+    repeats = [length if d == dim else 1 for d in range(value.ndim)]
+    return lax.all_to_all(
+        jnp.tile(value, repeats), axis, split_axis=dim, concat_axis=dim, tiled=True
+    )
 
 
 def entering(x, axis, join, neutral):
@@ -114,9 +122,7 @@
     scaling = lax.rsqrt(squares / (head_count * head_dim * n_exp) + eps_norm)
     normed_mix = (gated_out * scaling[:, None] * norm_gain[None, :]).astype(jnp.bfloat16)
     partial_value = jnp.dot(
-        normed_mix,
-        lax.all_gather(out_proj, "ctx", axis=1, tiled=True),
-        preferred_element_type=jnp.float32,
+        normed_mix, tiled_gather(out_proj, "ctx", 1), preferred_element_type=jnp.float32
     )
     gate_rows = w_gate[0]
     up_rows = w_up[0]

time: 696 us -> 787 us (1.13)
  waiting for transfers between devices: 439 us -> 499 us
  local copies, waits for them, and re-layouts: 52.4 us -> 70.2 us
  starting transfers between devices: 8.55 us -> 18.6 us
    all_to_all x0 -> x1, waiting for transfers between devices: none -> 122 us  [tiled_gather(): lax.all_to_all(jnp.tile(value, repeats), axis, split_axis=dim, concat_axi...]
    all_gather x1, waiting for transfers between devices: 55.4 us -> 0.01 us  [entering(): gathered = lax.all_gather(packed.astype(jnp.bfloat16), axis)]
    all_gather x1 -> x0, waiting for transfers between devices: 37.1 us -> none  [local(): lax.all_gather(out_proj, 'ctx', axis=1, tiled=True)]
    psum x1, waiting for transfers between devices: 240 us -> 272 us  [local(): lax.psum(partial_value.astype(jnp.bfloat16), 'exp').astype(jnp.float32)]
    all_to_all x0 -> x1, local copies, waits for them, and re-layouts: none -> 11.9 us  [tiled_gather(): lax.all_to_all(jnp.tile(value, repeats), axis, split_axis=dim, concat_axi...]
    all_to_all x0 -> x1, starting transfers between devices: none -> 9.79 us  [tiled_gather(): lax.all_to_all(jnp.tile(value, repeats), axis, split_axis=dim, concat_axi...]
    unnamed x5 -> x4, waiting for transfers between devices: 78.5 us -> 77.8 us
  transfers between devices with their start and end apart: 5 -> 5, of which waited for: 5 -> 4; matrix products, arithmetic and copies ran while one was open for 3% -> 3% of each run, Pallas kernels for 0% -> 0%
where the time goes in v1:
time: 787 us; the launch traced here: 777 us
  waiting for transfers between devices  499 us (63%)
  blocking collectives  113 us (14%)
  local copies, waits for them, and re-layouts  70.2 us (9%)
  matrix products  44.3 us (6%)
  starting transfers between devices  18.6 us (2%)
  other arithmetic  17.9 us (2%)
  between operations  14 us (2%)
    psum x1, waiting for transfers between devices, local(): lax.psum(partial_value.astype(jnp.bfloat16), 'exp').astype(jnp.float32)  272 us
    all_to_all x1, waiting for transfers between devices, tiled_gather(): lax.all_to_all(jnp.tile(value, repeats), axis, split_axis=dim, concat_axi...  122 us
    all_to_all x1, blocking collectives, local(): lax.all_to_all(outgoing, 'ctx', split_axis=1, concat_axis=1, tiled=True)  105 us
    unnamed x4, waiting for transfers between devices  77.8 us
    all_to_all x1, waiting for transfers between devices, local(): lax.all_to_all(summed, 'ctx', split_axis=1, concat_axis=1, tiled=True)  27.1 us
  transfers between devices with their start and end apart: 5, of which 4 were waited for; matrix products, arithmetic and copies ran while one was open for 3% of the time, Pallas kernels for 0%

profile of v1, /device:TPU:1, one launch (start us, length us, event | category | flops | bytes accessed | tf_op | source)
XLA Modules:
  0.0 777.4 jit_solution(6239854454344536156)
XLA Ops:
  11.0 6.1 tile.2
  17.0 9.8 %all-to-all-start = ((bf16[1024,32,128]{2,0,1:T(8,128)(2,1)}), bf16[1024,32,128]{2,0,1:T(8,128)(2,1)}, u32[]{:S(2)}, u32[]{:S(2)}) async-start(bf16[1024,32,128]{2,0,1:T(8,128)(2,1)} %tile.2), calls=%async_computation | async-start | bytes 16777216 | tf_op jit(solution)/shard_map/all_to_all | solution.py:14
  27.0 121.5 %all-to-all-done = bf16[1024,32,128]{2,0,1:T(8,128)(2,1)} async-done(((bf16[1024,32,128]{2,0,1:T(8,128)(2,1)}), bf16[1024,32,128]{2,0,1:T(8,128)(2,1)}, u32[]{:S(2)}, u32[]{:S(2)}) %all-to-all-start) | async-done | bytes 8388640 | tf_op jit(solution)/shard_map/all_to_all | solution.py:14
  148.5 11.9 %copy.120 = bf16[1024,32,128]{0,2,1:T(8,128)(2,1)} copy(bf16[1024,32,128]{2,0,1:T(8,128)(2,1)} %all-to-all-done) | data formatting | bytes 16777216 | tf_op jit(solution)/shard_map/all_to_all | solution.py:14
  160.5 2.5 broadcast_in_dim.28
  162.9 7.9 %while.12 = (s32[]{:T(128)}, f32[16]{0:T(128)S(1)}, f32[16,64,128]{0,2,1:T(8,128)}, s32[]{:T(128)}, bf16[32,16,65,128]{3,1,2,0:T(8,128)(2,1)}, /*index=5*/s32[]{:T(128)}, s32[]{:T(128)}, s32[]{:T(128)}) while((s32[]{:T(128)}, f32[16]{0:T(128)S(1)}, f32[16,64,128]{0,2,1:T(8,128)}, s32[]{:T(128)}, bf16[32,16,65,128]{3,1,2,0:T(8,128)(2,1)}, ...), condition=%wide.region_2.3_spmd, body=%wide.region_1.2_spmd.sunk | while | flops 395285 | bytes 3437051 | solution.py:32
  163.9 1.4 copy.137
  165.9 5.0 slice_add_fusion.2
  170.9 2.9 copy.116
  174.3 1.4 fusion.9
  176.2 8.5 %psum.14 = f32[128]{0:T(128)S(1)} all-reduce(f32[128]{0:T(128)S(1)} %multiply_reduce_fusion.2), channel_id=1, replica_groups=mesh['ctx'=32,'exp'=4] {'exp'}, use_global_device_ids=true, to_apply=%region_4.5 | all-reduce | flops 128 | bytes 1024 | tf_op jit(solution)/shard_map/psum | solution.py:121
  184.7 7.5 convolution_convert_fusion.2
  193.5 272.4 %all-reduce.2.cloned.1.call-done = bf16[128,4096]{1,0:T(8,128)(2,1)} async-done(((bf16[128,4096]{1,0:T(8,128)(2,1)}), bf16[128,4096]{1,0:T(8,128)(2,1)}) %all-reduce.2.cloned.1.call-update) | async-done | bytes 1048592 | tf_op jit(solution)/shard_map/psum | solution.py:134
  465.9 3.0 convert_add_fusion
  469.3 3.4 broadcast_in_dim.30
  472.7 2.7 reshape.170
  475.5 1.4 convolution_convert_fusion.1
  476.8 2.3 copy.122
  479.2 4.3 broadcast_in_dim.31
  483.4 104.9 %all_to_all.19 = bf16[32,32,4096]{2,0,1:T(8,128)(2,1)} all-to-all(bf16[32,32,4096]{2,0,1:T(8,128)(2,1)} %bitcast.71), channel_id=1, replica_groups=mesh['ctx'=32,'exp'=4] {'ctx'}, dimensions={1} | all-to-all | bytes 16777216 | tf_op jit(solution)/shard_map/all_to_all | solution.py:147
  588.4 11.3 %copy.123 = bf16[32,32,4096]{2,1,0:T(8,128)(2,1)} copy(bf16[32,32,4096]{2,0,1:T(8,128)(2,1)} %all_to_all.19) | data formatting | bytes 16777216 | tf_op jit(solution)/shard_map/all_to_all | solution.py:147
  599.7 12.7 %fusion.2 = f32[1024,896]{1,0:T(8,128)S(1)} fusion(bf16[1024,4096]{1,0:T(8,128)(2,1)} %bitcast.74, bf16[1,4096,896]{2,1,0:T(8,128)(2,1)} %param.32), kind=kOutput, calls=%fused_computation.8 | convolution fusion | flops 7516192768 | bytes 19398656 | tf_op jit(solution)/shard_map/dot_general | solution.py:150
  612.5 9.2 %multiply_convert_fusion = bf16[1024,896]{1,0:T(8,128)(2,1)S(1)} fusion(f32[1024,896]{1,0:T(8,128)S(1)} %fusion.2, bf16[1024,4096]{1,0:T(8,128)(2,1)S(1)} %bitcast.75, bf16[1,4096,896]{2,1,0:T(8,128)(2,1)S(1)} %bitcast.83), kind=kOutput, calls=%fused_computation.14 | convolution fusion | flops 7521697792 | bytes 21233664 | tf_op jit(solution)/shard_map/dot_general | solution.py:149
  621.7 11.3 %convolution_convert_fusion = bf16[1024,4096]{1,0:T(8,128)(2,1)} fusion(bf16[1024,896]{1,0:T(8,128)(2,1)S(1)} %multiply_convert_fusion, bf16[1,896,4096]{2,1,0:T(8,128)(2,1)S(1)} %bitcast.85), kind=kOutput, calls=%fused_computation.6 | convolution fusion | flops 7520387072 | bytes 17563648 | tf_op jit(solution)/shard_map/dot_general | solution.py:154
  633.0 11.3 %copy.135 = bf16[4,8,32,4096]{3,1,2,0:T(8,128)(2,1)} copy(bf16[4,8,32,4096]{3,2,1,0:T(8,128)(2,1)} %bitcast.76) | data formatting | bytes 16777216
  644.3 77.8 %reduce-scatter.4.cloned.1.call-done = bf16[8,131072]{1,0:T(8,128)(2,1)} async-done(((bf16[32,131072]{1,0:T(8,128)(2,1)}), bf16[8,131072]{1,0:T(8,128)(2,1)}) %reduce-scatter.4.cloned.1.call-update) | async-done | bytes 2097168
  722.1 8.2 %all-to-all-start.2 = ((bf16[8,32,4096]{2,0,1:T(8,128)(2,1)}), bf16[8,32,4096]{2,0,1:T(8,128)(2,1)}, u32[]{:S(2)}, u32[]{:S(2)}) async-start(bf16[8,32,4096]{2,0,1:T(8,128)(2,1)} %bitcast.78), calls=%async_computation.2 | async-start | bytes 4194304 | tf_op jit(solution)/shard_map/all_to_all | solution.py:166
  731.3 27.1 %all-to-all-done.2 = bf16[8,32,4096]{2,0,1:T(8,128)(2,1)} async-done(((bf16[8,32,4096]{2,0,1:T(8,128)(2,1)}), bf16[8,32,4096]{2,0,1:T(8,128)(2,1)}, u32[]{:S(2)}, u32[]{:S(2)}) %all-to-all-start.2) | async-done | bytes 2097184 | tf_op jit(solution)/shard_map/all_to_all | solution.py:166
  758.4 2.7 copy.125
  763.7 2.7 reduce_sum.60
  767.0 1.4 multiply_reduce_fusion.1
  768.5 1.8 add_convert_fusion
  (88 shorter events, 12.9 us)
Async XLA Ops:
  6.5 3.1 copy-start
  6.5 153.9 %all-gather.2.cloned.1.call-start = ((), (), s32[]{:S(2)}) async-start(), calls=%async_computation.4 | async-start | bytes 8785920 | tf_op jit(solution)/shard_map/all_gather | solution.py:25
  17.0 9.9 %copy-start.7 = (bf16[128,128]{1,0:T(8,128)(2,1)S(1)}, bf16[128,128]{1,0:T(8,128)(2,1)}, u32[]{:S(2)}) copy-start(bf16[128,128]{1,0:T(8,128)(2,1)} %param.22) | copy-start | bytes 98308
  17.0 131.5 %all-to-all-start = ((bf16[1024,32,128]{2,0,1:T(8,128)(2,1)}), bf16[1024,32,128]{2,0,1:T(8,128)(2,1)}, u32[]{:S(2)}, u32[]{:S(2)}) async-start(bf16[1024,32,128]{2,0,1:T(8,128)(2,1)} %tile.2), calls=%async_computation | async-start | bytes 16777216 | tf_op jit(solution)/shard_map/all_to_all | solution.py:14
  26.8 439.0 %all-reduce.2.cloned.1.call-start = ((), (), s32[]{:S(2)}) async-start(), calls=%async_computation.5 | async-start | bytes 2097152 | tf_op jit(solution)/shard_map/psum | solution.py:134
  170.8 3.0 copy-start.5
  170.8 3.5 copy-start.9
  170.8 3.5 copy-start.13
  170.9 5.1 copy-start.6
  173.8 10.9 %copy-start.12 = (f32[1024]{0:T(1024)S(1)}, f32[1024]{0:T(1024)}, u32[]{:S(2)}) copy-start(f32[1024]{0:T(1024)} %param.27) | copy-start | bytes 12292
  184.7 8.1 %copy-start.10 = (s32[128,2]{0,1:T(2,128)S(1)}, s32[128,2]{0,1:T(2,128)}, u32[]{:S(2)}) copy-start(s32[128,2]{0,1:T(2,128)} %param.34) | copy-start | bytes 3076
  184.7 281.1 %copy-start.3 = (bf16[128,4096]{1,0:T(8,128)(2,1)S(1)}, bf16[128,4096]{1,0:T(8,128)(2,1)}, u32[]{:S(2)}) copy-start(bf16[128,4096]{1,0:T(8,128)(2,1)} %param.29) | copy-start | bytes 3145732
  192.2 276.7 %copy-start.8 = (f32[4096]{0:T(1024)S(1)}, f32[4096]{0:T(1024)}, u32[]{:S(2)}) copy-start(f32[4096]{0:T(1024)} %param.30) | copy-start | bytes 49156
  192.2 529.9 %reduce-scatter.4.cloned.1.call-start = ((), (), s32[]{:S(2)}) async-start(), calls=%async_computation.6 | async-start | bytes 10485760
  465.9 3.0 copy-start.4
  588.4 24.0 %slice-start = ((s8[7340032]{0:T(1024)(128)(4,1)}), s8[3145728]{0:T(1024)(128)(4,1)S(1)}, s32[]{:S(2)}) async-start(s8[7340032]{0:T(1024)(128)(4,1)} %bitcast.82), calls=%async_computation.7 | async-start | bytes 6291456
  599.7 12.7 %copy-start.2 = (bf16[32,32,4096]{2,1,0:T(8,128)(2,1)S(1)}, bf16[32,32,4096]{2,1,0:T(8,128)(2,1)}, u32[]{:S(2)}) copy-start(bf16[32,32,4096]{2,1,0:T(8,128)(2,1)} %copy.123) | copy-start | bytes 25165828
  599.7 12.7 %slice-start.1 = ((s8[7340032]{0:T(1024)(128)(4,1)}), s8[4194304]{0:T(1024)(128)(4,1)S(1)}, s32[]{:S(2)}) async-start(s8[7340032]{0:T(1024)(128)(4,1)} %bitcast.82), calls=%async_computation.8 | async-start | bytes 8388608
  599.7 21.9 %slice-start.2 = ((s8[7340032]{0:T(1024)(128)(4,1)}), s8[4194304]{0:T(1024)(128)(4,1)S(1)}, s32[]{:S(2)}) async-start(s8[7340032]{0:T(1024)(128)(4,1)} %bitcast.84), calls=%async_computation.9 | async-start | bytes 8388608
  612.4 9.2 %slice-start.3 = ((s8[7340032]{0:T(1024)(128)(4,1)}), s8[3145728]{0:T(1024)(128)(4,1)S(1)}, s32[]{:S(2)}) async-start(s8[7340032]{0:T(1024)(128)(4,1)} %bitcast.84), calls=%async_computation.10 | async-start | bytes 6291456
  644.3 86.8 %copy-start.11 = (f32[128,2]{0,1:T(2,128)S(1)}, f32[128,2]{0,1:T(2,128)}, u32[]{:S(2)}) copy-start(f32[128,2]{0,1:T(2,128)} %param.35) | copy-start | bytes 3076
  722.1 36.3 %all-to-all-start.2 = ((bf16[8,32,4096]{2,0,1:T(8,128)(2,1)}), bf16[8,32,4096]{2,0,1:T(8,128)(2,1)}, u32[]{:S(2)}, u32[]{:S(2)}) async-start(bf16[8,32,4096]{2,0,1:T(8,128)(2,1)} %bitcast.78), calls=%async_computation.2 | async-start | bytes 4194304 | tf_op jit(solution)/shard_map/all_to_all | solution.py:166
  762.3 8.0 %copy-start.1 = (bf16[128,128]{1,0:T(8,128)(2,1)S(1)}, bf16[128,128]{1,0:T(8,128)(2,1)}, u32[]{:S(2)}) copy-start(bf16[128,128]{1,0:T(8,128)(2,1)} %param.21) | copy-start | bytes 98308
Sparse Core Ops, SparseCore 0:
  11.1 131.2 all-gather.1
  192.3 273.4 all-reduce.1
  644.4 77.6 reduce-scatter.3
